TPU v7x, 768 devices: a whole 4x8x12 slice. The times are simulated.
768 devices in a mesh: users: 192 (over y, z, core), items: 4 (over x).
Axes of the slice: x: 4, y: 8, z: 12, core: 2. Of those that a mesh axis runs over, the one named last changes fastest.
Arguments:
- ratings: bfloat16 [192, 4, 8, 256, 256], P('users', 'items'), may hold values from -6 to 6
- confidence: bfloat16 [192, 4, 8, 256, 256], P('users', 'items'), may hold values from 0 to 2, as said below
- tile_user: int32 [192, 4, 8], P('users', 'items'), may hold values from 0 to 3, as said below
- tile_item: int32 [192, 4, 8], P('users', 'items'), may hold values from 0 to 2, as said below
- tile_count: int32 [192, 4], P('users', 'items'), may hold values from 1 to 8, as said below
- user_factor: bfloat16 [196608, 256], P('users'), may hold values from -1.5 to 1.5
- user_linear: float32 [196608, 256], P('users'), may hold values from -6 to 6
- user_squares: float32 [196608, 256], P('users'), may hold values from 0.25 to 4
- item_factor: bfloat16 [3072, 256], P('items'), may hold values from -1.5 to 1.5
- item_linear: float32 [3072, 256], P('items'), may hold values from -6 to 6
- item_squares: float32 [3072, 256], P('items'), may hold values from 0.25 to 4
Outputs:
- new_user_factor: bfloat16 [196608, 256], P('users')
- new_user_linear: float32 [196608, 256], P('users')
- new_user_squares: float32 [196608, 256], P('users')
- new_item_factor: bfloat16 [3072, 256], P('items')
- new_item_linear: float32 [3072, 256], P('items')
- new_item_squares: float32 [3072, 256], P('items')
Inputs may be any that keep to these rules, and one draw needn't show every extreme that they name: Within one device no pair (tile_user, tile_item) occurs twice among its 8 slots. Within one device no pair (tile_user, tile_item) occurs twice among its 8 slots. `tile_count`: some device has all 8 slots live. `confidence`: each entry is zero or at least 0.25.
All inputs are finite; a program needn't handle non-finite values.
Results may differ from a plain program's by a relative error of at most 0.0028.
Values sent between devices are 32-bit elements; how exact they have to be, the bound alone decides.
A program may use at most 32 MiB of HBM per device.

v0:
```python
import jax
import jax.numpy as jnp
from jax import lax
from jax.sharding import PartitionSpec as P

learn_alpha = 0.25
beta_offset = 1.0
lasso_weight = 0.5
ridge_weight = 1.0


def ftrl_state(gradient, linear, squares, factor):
    new_squares = squares + gradient * gradient
    sigma_step = (jnp.sqrt(new_squares) - jnp.sqrt(squares)) / learn_alpha
    new_linear = linear + gradient - sigma_step * factor.astype(jnp.float32)
    return (new_linear, new_squares)


def ftrl_factor(linear, squares):
    shrink = linear - lasso_weight * jnp.sign(linear)
    denominator = (beta_offset + jnp.sqrt(squares)) / learn_alpha + ridge_weight
    weight = jnp.where(
        jnp.abs(linear) <= lasso_weight, jnp.zeros_like(linear), -shrink / denominator
    )
    return weight.astype(jnp.bfloat16)


def pick_blocks(onehot, blocks):
    return jnp.einsum("tk,kar->tar", onehot, blocks, preferred_element_type=jnp.float32).astype(
        jnp.bfloat16
    )


def tile_error(user_tiles, item_tiles, live_mask, confidence, ratings):
    predict = jnp.einsum("tar,tbr->tab", user_tiles, item_tiles, preferred_element_type=jnp.float32)
    error = (
        live_mask[:, None, None]
        * confidence.astype(jnp.float32)
        * (predict - ratings.astype(jnp.float32))
    )
    return error.astype(jnp.bfloat16)


def on_device(
    ratings,
    confidence,
    tile_user,
    tile_item,
    tile_count,
    user_factor,
    user_linear,
    user_squares,
    item_factor,
    item_linear,
    item_squares,
):
    slot_count = ratings.shape[2]
    tile_width = ratings.shape[3]
    rank_width = user_factor.shape[1]
    user_blocks = user_factor.shape[0] // tile_width
    item_blocks = item_factor.shape[0] // tile_width
    ratings = ratings.reshape(slot_count, tile_width, tile_width)
    confidence = confidence.reshape(slot_count, tile_width, tile_width)
    live_mask = (jnp.arange(slot_count, dtype=jnp.int32) < tile_count.reshape(())).astype(
        jnp.float32
    )
    user_pick = (
        tile_user.reshape(slot_count)[:, None] == jnp.arange(user_blocks, dtype=jnp.int32)[None, :]
    )
    item_pick = (
        tile_item.reshape(slot_count)[:, None] == jnp.arange(item_blocks, dtype=jnp.int32)[None, :]
    )
    item_tiles = pick_blocks(
        item_pick.astype(jnp.bfloat16), item_factor.reshape(item_blocks, tile_width, rank_width)
    )
    user_tiles = pick_blocks(
        user_pick.astype(jnp.bfloat16), user_factor.reshape(user_blocks, tile_width, rank_width)
    )
    error = tile_error(user_tiles, item_tiles, live_mask, confidence, ratings)
    per_tile = jnp.einsum("tab,tbr->tar", error, item_tiles, preferred_element_type=jnp.float32)
    user_partial = jnp.einsum(
        "tk,tar->kar", user_pick.astype(jnp.float32), per_tile, precision=lax.Precision.HIGHEST
    )
    user_grad = lax.psum(
        user_partial.reshape(user_blocks * tile_width, rank_width), "items"
    ) * tile_width ** (-0.5)
    new_user_linear, new_user_squares = ftrl_state(
        user_grad, user_linear, user_squares, user_factor
    )
    new_user_factor = ftrl_factor(new_user_linear, new_user_squares)
    users_fresh = pick_blocks(
        user_pick.astype(jnp.bfloat16), new_user_factor.reshape(user_blocks, tile_width, rank_width)
    )
    error_second = tile_error(users_fresh, item_tiles, live_mask, confidence, ratings)
    per_item = jnp.einsum(
        "tab,tar->tbr", error_second, users_fresh, preferred_element_type=jnp.float32
    )
    item_partial = jnp.einsum(
        "tk,tbr->kbr", item_pick.astype(jnp.float32), per_item, precision=lax.Precision.HIGHEST
    )
    item_partial = item_partial.reshape(item_blocks * tile_width, rank_width)
    item_scale = (tile_width * lax.axis_size("users")) ** (-0.5)
    grad_share = (
        lax.psum_scatter(item_partial, "users", scatter_dimension=0, tiled=True) * item_scale
    )
    share_rows = grad_share.shape[0]
    row_start = lax.axis_index("users") * share_rows
    linear_share = lax.dynamic_slice_in_dim(item_linear, row_start, share_rows, 0)
    squares_share = lax.dynamic_slice_in_dim(item_squares, row_start, share_rows, 0)
    factor_share = lax.dynamic_slice_in_dim(item_factor, row_start, share_rows, 0)
    linear_part, squares_part = ftrl_state(grad_share, linear_share, squares_share, factor_share)
    new_item_linear, new_item_squares = (
        lax.all_gather(linear_part, "users", axis=0, tiled=True),
        lax.all_gather(squares_part, "users", axis=0, tiled=True),
    )
    new_item_factor = ftrl_factor(new_item_linear, new_item_squares)
    return (
        new_user_factor,
        new_user_linear,
        new_user_squares,
        new_item_factor,
        new_item_linear,
        new_item_squares,
    )


def solution(mesh):
    placed = (
        P("users", "items", None, None, None),
        P("users", "items", None, None, None),
        P("users", "items", None),
        P("users", "items", None),
        P("users", "items"),
        P("users", None),
        P("users", None),
        P("users", None),
        P("items", None),
        P("items", None),
        P("items", None),
    )
    return jax.shard_map(
        on_device,
        mesh=mesh,
        in_specs=placed,
        out_specs=(
            P("users", None),
            P("users", None),
            P("users", None),
            P("items", None),
            P("items", None),
            P("items", None),
        ),
        check_vma=False,
    )
```

profile of v0, /device:TPU:1, one launch (start us, length us, event | category | flops | bytes accessed | tf_op | source)
XLA Modules:
  0.0 544.9 jit_solution(497887569852039427)
XLA Ops:
  7.2 0.0 all-reduce.4.cloned.1.call-start
  7.9 1.5 convolution_convert_fusion.1
  9.4 0.0 copy-start.4
  9.4 3.0 convolution_convert_fusion.2
  12.4 0.0 copy-start.7
  12.4 3.0 fusion.9
  15.4 0.0 copy-done.4
  15.4 0.0 copy-done.7
  15.4 2.2 fusion.6
  17.7 0.0 copy-start.2
  17.7 0.0 copy-start.5
  17.7 0.0 copy-start.6
  17.7 1.2 copy.29
  18.9 0.0 all-reduce.4.cloned.1.call-update
  18.9 0.0 all-reduce.6.cloned.1.call-start
  18.9 68.3 %all-reduce.4.cloned.1.call-done = f32[1024,256]{1,0:T(8,128)} async-done(((f32[1024,256]{1,0:T(8,128)}), f32[1024,256]{1,0:T(8,128)}) %all-reduce.4.cloned.1.call-update) | async-done | bytes 1048592 | tf_op jit(solution)/shard_map/psum | solution.py:84
  87.2 0.0 copy-done.2
  87.2 0.0 copy-done.5
  87.2 0.0 copy-done.6
  87.2 4.0 select_convert_fusion
  91.2 0.0 copy-start.3
  91.2 1.6 convolution_convert_fusion
  92.8 0.0 copy-start.8
  92.8 3.6 fusion.8
  96.4 0.0 copy-done.3
  96.5 0.0 copy-done.8
  96.5 2.2 fusion.4
  98.7 1.0 copy.36
  99.7 0.0 all-reduce.6.cloned.1.call-update
  99.7 1.3 dynamic-slice
  101.7 297.3 %all-reduce.6.cloned.1.call-done = f32[768,256]{1,0:T(8,128)} async-done(((f32[768,256]{1,0:T(8,128)}), f32[768,256]{1,0:T(8,128)}) %all-reduce.6.cloned.1.call-update) | async-done | bytes 786448
  399.0 0.8 subtract_bitcast_fusion
  399.7 69.2 %all-gather = f32[192,4,256]{2,1,0:T(4,128)S(1)} all-gather(f32[1,4,256]{2,1,0:T(4,128)S(1)} %get-tuple-element.9), channel_id=1, replica_groups=mesh['users'=192,'items'=4] {'users'}, dimensions={0}, use_global_device_ids=true | all-gather | bytes 790528 | tf_op jit(solution)/shard_map/all_gather | solution.py:113
  469.0 0.3 reshape.52
  469.2 0.0 copy-start
  469.2 67.1 %all-gather.1 = f32[192,4,256]{2,1,0:T(4,128)S(1)} all-gather(f32[1,4,256]{2,1,0:T(4,128)S(1)} %get-tuple-element.10), channel_id=1, replica_groups=mesh['users'=192,'items'=4] {'users'}, dimensions={0}, use_global_device_ids=true | all-gather | bytes 790528 | tf_op jit(solution)/shard_map/all_gather | solution.py:114
  536.3 0.3 reshape.54
  536.6 0.0 copy-start.1
  536.6 1.4 select_convert_fusion.1
  538.1 0.0 copy-done
  538.1 0.0 copy-done.1
  (1 shorter events, 0.0 us)
Async XLA Ops:
  7.2 80.0 %all-reduce.4.cloned.1.call-start = ((), (), s32[]{:S(2)}) async-start(), calls=%async_computation | async-start | bytes 2097152 | tf_op jit(solution)/shard_map/psum | solution.py:84
  9.4 6.0 %copy-start.4 = (bf16[8,256,256]{2,0,1:T(8,128)(2,1)}, bf16[8,256,256]{2,0,1:T(8,128)(2,1)S(1)}, u32[]{:S(2)}) copy-start(bf16[8,256,256]{2,0,1:T(8,128)(2,1)S(1)} %convolution_convert_fusion.1) | copy-start | bytes 3145732
  12.4 3.0 copy-start.7
  17.7 69.5 %copy-start.2 = (bf16[1024,256]{1,0:T(8,128)(2,1)S(1)}, bf16[1024,256]{1,0:T(8,128)(2,1)}, u32[]{:S(2)}) copy-start(bf16[1024,256]{1,0:T(8,128)(2,1)} %param.16) | copy-start | bytes 1572868
  17.7 69.5 %copy-start.5 = (f32[1024,256]{1,0:T(8,128)S(1)}, f32[1024,256]{1,0:T(8,128)}, u32[]{:S(2)}) copy-start(f32[1024,256]{1,0:T(8,128)} %param.18) | copy-start | bytes 3145732
  17.7 69.5 %copy-start.6 = (f32[1024,256]{1,0:T(8,128)S(1)}, f32[1024,256]{1,0:T(8,128)}, u32[]{:S(2)}) copy-start(f32[1024,256]{1,0:T(8,128)} %param.17) | copy-start | bytes 3145732
  18.9 380.1 %all-reduce.6.cloned.1.call-start = ((), (), s32[]{:S(2)}) async-start(), calls=%async_computation.1 | async-start | bytes 1572864
  91.2 5.2 copy-start.3
  92.8 3.7 copy-start.8
  469.2 68.8 %copy-start = (f32[768,256]{1,0:T(8,128)}, f32[768,256]{1,0:T(8,128)S(1)}, u32[]{:S(2)}) copy-start(f32[768,256]{1,0:T(8,128)S(1)} %reshape.52) | copy-start | bytes 2359300
  536.6 1.4 copy-start.1
Sparse Core Ops, SparseCore 0:
  19.0 68.1 all-reduce.3
  99.8 299.0 all-reduce.5
where the time goes:
time: 546 us; the launch traced here: 545 us
  waiting for transfers between devices  366 us (67%)
  blocking collectives  136 us (25%)
  matrix products  17.1 us (3%)
  between operations  15.5 us (3%)
  other arithmetic  6.21 us (1%)
    unnamed x3, waiting for transfers between devices  297 us
    all_gather x1, blocking collectives, on_device(): lax.all_gather(linear_part, 'users', axis=0, tiled=True)  69.2 us
    psum x1, waiting for transfers between devices, on_device(): lax.psum(user_partial.reshape(user_blocks * tile_width, rank_width), 'ite...  68.3 us
    all_gather x1, blocking collectives, on_device(): lax.all_gather(squares_part, 'users', axis=0, tiled=True)  67.1 us
  transfers between devices with their start and end apart: 2, of which 2 were waited for; matrix products, arithmetic and copies ran while one was open for 0% of the time, Pallas kernels for 0%

commit v1 on v0

v1 whole, which is shorter than its diff:
```python
import functools

import jax
import jax.numpy as jnp
from jax import lax
from jax.experimental import pallas as pl
from jax.experimental.pallas import tpu as pltpu
from jax.sharding import PartitionSpec as P

learn_alpha = 0.25
beta_offset = 1.0
lasso_weight = 0.5
ridge_weight = 1.0

ALONG_Z = 12
CORES = 2


def ftrl_state(gradient, linear, squares, factor):
    new_squares = squares + gradient * gradient
    sigma_step = (jnp.sqrt(new_squares) - jnp.sqrt(squares)) / learn_alpha
    new_linear = linear + gradient - sigma_step * factor.astype(jnp.float32)
    return (new_linear, new_squares)


def ftrl_factor(linear, squares):
    shrink = linear - lasso_weight * jnp.sign(linear)
    denominator = (beta_offset + jnp.sqrt(squares)) / learn_alpha + ridge_weight
    weight = jnp.where(
        jnp.abs(linear) <= lasso_weight, jnp.zeros_like(linear), -shrink / denominator
    )
    return weight.astype(jnp.bfloat16)


def slot_table(tile_user, tile_item, item_blocks):
    return [tile_user[t] * item_blocks + tile_item[t] for t in range(tile_user.shape[0])]


def slot_of(codes, count, pair):
    slot = jnp.int32(0)
    live = jnp.int32(0)
    for t, code in enumerate(codes):
        slot = jnp.where(code == pair, t, slot)
        live = jnp.where(code == pair, jnp.where(t < count, 1, 0), live)
    return slot, live.astype(jnp.float32)


def pair_error(user_rows, item_rows, ratings, confidence, live):
    predict = lax.dot_general(
        user_rows, item_rows, (((1,), (1,)), ((), ())), preferred_element_type=jnp.float32
    )
    error = live * confidence.astype(jnp.float32) * (predict - ratings.astype(jnp.float32))
    return error.astype(jnp.bfloat16)


def remote(source, target, send, receive, device):
    return pltpu.make_async_remote_copy(
        src_ref=source,
        dst_ref=target,
        send_sem=send,
        recv_sem=receive,
        device_id=device,
        device_id_type=pl.DeviceIdType.MESH,
    )


def user_kernel(
    tile_user,
    tile_item,
    tile_count,
    ratings,
    confidence,
    user_factor,
    item_factor,
    total,
    part,
    pass_right,
    pass_left,
    from_left,
    from_right,
    send,
    receive,
):
    user_blocks, width, rank = user_factor.shape
    item_blocks = item_factor.shape[0]
    half = width // 2
    n = lax.axis_size("items")
    me = lax.axis_index("items")
    right, left, far = lax.rem(me + 1, n), lax.rem(me + 3, n), lax.rem(me + 2, n)

    barrier = pltpu.get_barrier_semaphore()
    for other in (left, right):
        pl.semaphore_signal(
            barrier, inc=1, device_id={"items": other}, device_id_type=pl.DeviceIdType.MESH
        )

    codes = slot_table(tile_user, tile_item, item_blocks)
    count = tile_count[0]

    def block(k):
        rows = user_factor[k]
        gradient = jnp.zeros((width, rank), jnp.float32)
        for i in range(item_blocks):
            slot, live = slot_of(codes, count, k * item_blocks + i)
            error = pair_error(rows, item_factor[i], ratings[slot], confidence[slot], live)
            gradient += jnp.dot(error, item_factor[i], preferred_element_type=jnp.float32)
        part[k] = gradient

    low, high = pl.ds(0, half), pl.ds(half, half)

    block(far)
    pl.semaphore_wait(barrier, 2)
    copies = [
        remote(part.at[far, low], pass_right, send.at[0], receive.at[0], {"items": right}),
        remote(part.at[far, high], pass_left, send.at[1], receive.at[1], {"items": left}),
        remote(part.at[right, high], from_left.at[high], send.at[2], receive.at[2], {"items": right}),
        remote(part.at[left, low], from_right.at[low], send.at[3], receive.at[3], {"items": left}),
        remote(part.at[right, low], from_left.at[low], send.at[4], receive.at[4], {"items": right}),
        remote(part.at[left, high], from_right.at[high], send.at[5], receive.at[5], {"items": left}),
        remote(total.at[me, low], total.at[me, low], send.at[6], receive.at[6], {"items": right}),
        remote(total.at[me, high], total.at[me, high], send.at[7], receive.at[7], {"items": left}),
        remote(total.at[me, high], total.at[me, high], send.at[8], receive.at[8], {"items": right}),
        remote(total.at[me, low], total.at[me, low], send.at[9], receive.at[9], {"items": left}),
        remote(total.at[left, low], total.at[left, low], send.at[10], receive.at[10], {"items": right}),
        remote(total.at[right, high], total.at[right, high], send.at[11], receive.at[11], {"items": left}),
    ]
    copies[0].start()
    copies[1].start()
    block(right)
    copies[2].start()
    block(left)
    copies[3].start()
    copies[0].wait_recv()
    part[right, low] += pass_right[...]
    copies[1].wait_recv()
    part[left, high] += pass_left[...]
    copies[4].start()
    copies[5].start()
    block(me)
    copies[3].wait_recv()
    copies[4].wait_recv()
    total[me, low] = part[me, low] + (from_left[low] + from_right[low])
    copies[6].start()
    copies[2].wait_recv()
    copies[5].wait_recv()
    total[me, high] = part[me, high] + (from_left[high] + from_right[high])
    copies[7].start()
    copies[8].start()
    copies[9].start()
    copies[6].wait_recv()
    copies[10].start()
    copies[7].wait_recv()
    copies[11].start()
    for j in range(8, 12):
        copies[j].wait_recv()
    for j in range(12):
        copies[j].wait_send()


def item_kernel(
    along_z,
    tile_user,
    tile_item,
    tile_count,
    ratings,
    confidence,
    user_factor,
    item_factor,
    total,
    part,
    arrived,
    mine,
    chunk_sum,
    first_in,
    second_in,
    pair_sem,
    send_first,
    recv_first,
    send_second,
    recv_second,
    send_tile,
    recv_tile,
    send_chunk,
    recv_chunk,
    send_over,
    recv_over,
):
    user_blocks, width, rank = user_factor.shape
    item_blocks = item_factor.shape[0]
    half_rows = item_blocks * width // CORES
    along_y = lax.axis_size("users") // (along_z * CORES)
    me = lax.axis_index("users")
    core = lax.rem(me, CORES)
    z = lax.rem(me // CORES, along_z)
    y = me // (CORES * along_z)
    partner = me + 1 - 2 * core

    def at_y(t):
        return {"users": (t * along_z + z) * CORES + core}

    def at_z(t):
        return {"users": (y * along_z + t) * CORES + core}

    def greet(device):
        pl.semaphore_signal(
            barrier, inc=1, device_id=device, device_id_type=pl.DeviceIdType.MESH
        )

    barrier = pltpu.get_barrier_semaphore()
    greet({"users": partner})

    @pl.loop(1, along_y)
    def _(d):
        greet(at_y(lax.rem(y + d, along_y)))

    @pl.loop(1, along_z)
    def _(d):
        greet(at_z(lax.rem(z + d, along_z)))

    codes = slot_table(tile_user, tile_item, item_blocks)
    count = tile_count[0]

    def block(i):
        rows = item_factor[i]
        gradient = jnp.zeros((width, rank), jnp.float32)
        for k in range(user_blocks):
            slot, live = slot_of(codes, count, k * item_blocks + i)
            error = pair_error(user_factor[k], rows, ratings[slot], confidence[slot], live)
            gradient += lax.dot_general(
                error,
                user_factor[k],
                (((0,), (0,)), ((), ())),
                preferred_element_type=jnp.float32,
            )
        part[pl.ds(pl.multiple_of(i * width, width), width), :] = gradient

    own = pl.ds(pl.multiple_of(core * half_rows, half_rows), half_rows)
    theirs = pl.ds(pl.multiple_of((1 - core) * half_rows, half_rows), half_rows)
    block((item_blocks - 1) * (1 - core))
    block(1)
    pl.semaphore_wait(barrier, along_y + along_z - 1)
    swap = remote(part.at[theirs], arrived, pair_sem.at[0], pair_sem.at[1], {"users": partner})
    swap.start()
    block((item_blocks - 1) * core)
    swap.wait_recv()
    mine[...] = part[own, :] + arrived[...]

    def halves(base, n_first, first, at_first, n_second, second, at_second):
        chunk = half_rows // n_first

        def distance(n, j):
            step = (j + 1) // 2
            return n // 2 + step * (1 - 2 * lax.rem(j, 2))

        def rows_of(t):
            return pl.ds(pl.multiple_of(t * chunk, chunk), chunk)

        def out_rows(t):
            return pl.ds(pl.multiple_of(base + t * chunk, 8), chunk)

        def tile_of(t, start):
            return (
                pl.ds(pl.multiple_of(start + 8 * (t // 2), 8), 8),
                pl.ds(pl.multiple_of(128 * lax.rem(t, 2), 128), 128),
            )

        def to_first(j):
            t = lax.rem(first + distance(n_first, j), n_first)
            return remote(
                mine.at[rows_of(t)],
                first_in.at[j, pl.ds(0, chunk)],
                send_first.at[j],
                recv_first.at[j],
                at_first(t),
            )

        def to_second(j):
            t = lax.rem(second + distance(n_second, j), n_second)
            return remote(
                chunk_sum.at[tile_of(t, 0)],
                second_in.at[j],
                send_second.at[j],
                recv_second.at[j],
                at_second(t),
            )

        my_tile = tile_of(second, base + first * chunk)

        def tile_out(j):
            t = lax.rem(second + distance(n_second, j), n_second)
            return remote(
                total.at[my_tile], total.at[my_tile], send_tile.at[j], recv_tile.at[j], at_second(t)
            )

        def chunk_out(j):
            t = lax.rem(first + distance(n_first, j), n_first)
            return remote(
                total.at[out_rows(first)],
                total.at[out_rows(first)],
                send_chunk.at[j],
                recv_chunk.at[j],
                at_first(t),
            )

        def over(slot, t):
            return remote(
                total.at[out_rows(t)],
                total.at[out_rows(t)],
                send_over.at[slot],
                recv_over.at[slot],
                {"users": partner},
            )

        @pl.loop(0, n_first - 1)
        def _(j):
            to_first(j).start()

        def add_first(j, running):
            to_first(j).wait_recv()
            return running + first_in[j, pl.ds(0, chunk), :]

        chunk_sum[pl.ds(0, chunk), :] = lax.fori_loop(
            0, n_first - 1, add_first, mine[rows_of(first), :]
        )

        @pl.loop(0, n_second - 1)
        def _(j):
            to_second(j).start()

        def add_second(j, running):
            to_second(j).wait_recv()
            return running + second_in[j]

        total[my_tile] = lax.fori_loop(
            0, n_second - 1, add_second, chunk_sum[tile_of(second, 0)]
        )

        @pl.loop(0, n_second - 1)
        def _(j):
            tile_out(j).start()

        @pl.loop(0, n_second - 1)
        def _(j):
            tile_out(j).wait_recv()

        @pl.loop(0, n_first - 1)
        def _(j):
            chunk_out(j).start()

        over(n_first - 1, first).start()

        @pl.loop(0, n_first - 1)
        def _(j):
            chunk_out(j).wait_recv()
            over(j, lax.rem(first + n_first - distance(n_first, j), n_first)).start()

        @pl.loop(0, n_first - 1)
        def _(j):
            to_first(j).wait_send()
            chunk_out(j).wait_send()

        @pl.loop(0, n_second - 1)
        def _(j):
            to_second(j).wait_send()
            tile_out(j).wait_send()

        @pl.loop(0, n_first)
        def _(j):
            over(j, 0).wait_send()

        other_chunk = half_rows // n_second

        @pl.loop(0, n_second)
        def _(j):
            remote(
                total.at[pl.ds(0, other_chunk)],
                total.at[pl.ds(0, other_chunk)],
                send_over.at[j],
                recv_over.at[j],
                {"users": partner},
            ).wait_recv()

    @pl.when(core == 0)
    def _():
        halves(0, along_y, y, at_y, along_z, z, at_z)

    @pl.when(core == 1)
    def _():
        halves(half_rows, along_z, z, at_z, along_y, y, at_y)

    swap.wait_send()


VMEM = pl.BlockSpec(memory_space=pltpu.VMEM)
SMEM = pl.BlockSpec(memory_space=pltpu.SMEM)
IN_SPECS = [SMEM, SMEM, SMEM, VMEM, VMEM, VMEM, VMEM]
DMA = pltpu.SemaphoreType.DMA


def user_total(tiles, user_factor, item_factor):
    blocks, width, rank = user_factor.shape
    half = (width // 2, rank)
    return pl.pallas_call(
        user_kernel,
        name="user_total",
        out_shape=jax.ShapeDtypeStruct((blocks, width, rank), jnp.float32),
        in_specs=IN_SPECS,
        out_specs=VMEM,
        scratch_shapes=[
            pltpu.VMEM((blocks, width, rank), jnp.float32),
            pltpu.VMEM(half, jnp.float32),
            pltpu.VMEM(half, jnp.float32),
            pltpu.VMEM((width, rank), jnp.float32),
            pltpu.VMEM((width, rank), jnp.float32),
            DMA((12,)),
            DMA((12,)),
        ],
        compiler_params=pltpu.CompilerParams(
            collective_id=0, has_side_effects=True, vmem_limit_bytes=48 << 20
        ),
    )(*tiles, user_factor, item_factor)


def item_total(tiles, user_factor, item_factor, along_y, along_z):
    blocks, width, rank = item_factor.shape
    rows = blocks * width
    half_rows = rows // CORES
    most = max(along_y, along_z)
    chunk = half_rows // min(along_y, along_z)
    return pl.pallas_call(
        functools.partial(item_kernel, along_z),
        name="item_total",
        out_shape=jax.ShapeDtypeStruct((rows, rank), jnp.float32),
        in_specs=IN_SPECS,
        out_specs=VMEM,
        scratch_shapes=[
            pltpu.VMEM((rows, rank), jnp.float32),
            pltpu.VMEM((half_rows, rank), jnp.float32),
            pltpu.VMEM((half_rows, rank), jnp.float32),
            pltpu.VMEM((chunk, rank), jnp.float32),
            pltpu.VMEM((most - 1, chunk, rank), jnp.float32),
            pltpu.VMEM((most - 1, 8, 128), jnp.float32),
            DMA((2,)),
        ]
        + [DMA((most,))] * 10,
        compiler_params=pltpu.CompilerParams(
            collective_id=1, has_side_effects=True, vmem_limit_bytes=48 << 20
        ),
    )(*tiles, user_factor, item_factor)


def on_device(
    ratings,
    confidence,
    tile_user,
    tile_item,
    tile_count,
    user_factor,
    user_linear,
    user_squares,
    item_factor,
    item_linear,
    item_squares,
):
    slot_count = ratings.shape[2]
    width = ratings.shape[3]
    rank = user_factor.shape[1]
    user_blocks = user_factor.shape[0] // width
    item_blocks = item_factor.shape[0] // width
    user_devices = lax.axis_size("users")
    tiles = (
        tile_user.reshape(slot_count),
        tile_item.reshape(slot_count),
        tile_count.reshape(1),
        ratings.reshape(slot_count, width, width),
        confidence.reshape(slot_count, width, width),
    )
    items = item_factor.reshape(item_blocks, width, rank)
    user_sum = user_total(tiles, user_factor.reshape(user_blocks, width, rank), items)
    user_grad = user_sum.reshape(user_blocks * width, rank) * width ** (-0.5)
    new_user_linear, new_user_squares = ftrl_state(
        user_grad, user_linear, user_squares, user_factor
    )
    new_user_factor = ftrl_factor(new_user_linear, new_user_squares)
    item_sum = item_total(
        tiles,
        new_user_factor.reshape(user_blocks, width, rank),
        items,
        user_devices // (ALONG_Z * CORES),
        ALONG_Z,
    )
    item_grad = item_sum * (width * user_devices) ** (-0.5)
    new_item_linear, new_item_squares = ftrl_state(
        item_grad, item_linear, item_squares, item_factor
    )
    new_item_factor = ftrl_factor(new_item_linear, new_item_squares)
    return (
        new_user_factor,
        new_user_linear,
        new_user_squares,
        new_item_factor,
        new_item_linear,
        new_item_squares,
    )


def solution(mesh):
    placed = (
        P("users", "items", None, None, None),
        P("users", "items", None, None, None),
        P("users", "items", None),
        P("users", "items", None),
        P("users", "items"),
        P("users", None),
        P("users", None),
        P("users", None),
        P("items", None),
        P("items", None),
        P("items", None),
    )
    return jax.shard_map(
        on_device,
        mesh=mesh,
        in_specs=placed,
        out_specs=(
            P("users", None),
            P("users", None),
            P("users", None),
            P("items", None),
            P("items", None),
            P("items", None),
        ),
        check_vma=False,
    )
```

time: 546 us -> 85.3 us (0.16)
  waiting for transfers between devices: 366 us -> 0 us
  blocking collectives: 136 us -> 0 us
  Pallas kernels: 0 us -> 72.4 us
  matrix products: 17.1 us -> 0 us
  between operations: 15.5 us -> 1.38 us
    unnamed x3 -> x0, waiting for transfers between devices: 297 us -> none
    all_gather x2 -> x0, blocking collectives: 136 us -> none  [the longest x1 69.2 us: on_device(): lax.all_gather(linear_part, 'users', axis=0, tiled=True)]
    pallas_call x0 -> x2, Pallas kernels: none -> 72.4 us  [the longest x1 49.1 us: item_total(): pl.pallas_call(functools.partial(item_kernel, along_z), name='item_total'...]
    psum x1 -> x0, waiting for transfers between devices: 68.3 us -> none  [on_device(): lax.psum(user_partial.reshape(user_blocks * tile_width, rank_width), 'ite...]
    dot_general x7 -> x0, matrix products: 17.1 us -> none  [the longest x3 6.09 us: pick_blocks(): jnp.einsum('tk,kar->tar', onehot, blocks, preferred_element_type=jnp.floa...]
  transfers between devices with their start and end apart: 2 -> 0, of which waited for: 2 -> 0; matrix products, arithmetic and copies ran while one was open for 0% -> 0% of each run, Pallas kernels for 0% -> 0%
where the time goes in v1:
time: 85.3 us; the launch traced here: 85 us
  Pallas kernels  72.4 us (85%)
  local copies, waits for them, and re-layouts  6.44 us (8%)
  other arithmetic  4.72 us (6%)
  between operations  1.38 us (2%)
    pallas_call x1, Pallas kernels, item_total(): pl.pallas_call(functools.partial(item_kernel, along_z), name='item_total'...  49.1 us
    pallas_call x1, Pallas kernels, user_total(): pl.pallas_call(user_kernel, name='user_total', out_shape=jax.ShapeDtypeSt...  23.3 us
    unnamed x26, local copies, waits for them, and re-layouts  6.44 us
    convert_element_type x2, other arithmetic, ftrl_factor(): return weight.astype(jnp.bfloat16)  4.64 us

profile of v1, /device:TPU:1, one launch (start us, length us, event | category | flops | bytes accessed | tf_op | source)
XLA Modules:
  0.0 85.0 jit_solution(7504358725478148210)
XLA Ops:
  1.3 0.0 copy-start.7
  1.3 0.0 copy-start.8
  1.3 0.6 copy-done.7
  1.9 0.0 copy-done.8
  2.0 0.0 copy-start
  2.0 1.2 %copy-done = bf16[1,1,8,256,256]{4,3,2,1,0:T(8,128)(2,1)S(1)} copy-done((bf16[1,1,8,256,256]{4,3,2,1,0:T(8,128)(2,1)S(1)}, bf16[1,1,8,256,256]{4,3,2,1,0:T(8,128)(2,1)}, u32[]{:S(2)}) %copy-start) | copy-done | bytes 1048600
  3.2 0.0 copy-start.1
  3.2 1.2 %copy-done.1 = bf16[1,1,8,256,256]{4,3,2,1,0:T(8,128)(2,1)S(1)} copy-done((bf16[1,1,8,256,256]{4,3,2,1,0:T(8,128)(2,1)S(1)}, bf16[1,1,8,256,256]{4,3,2,1,0:T(8,128)(2,1)}, u32[]{:S(2)}) %copy-start.1) | copy-done | bytes 1048600
  4.4 0.0 copy-start.2
  4.4 1.0 %copy-done.2 = bf16[768,256]{1,0:T(8,128)(2,1)S(1)} copy-done((bf16[768,256]{1,0:T(8,128)(2,1)S(1)}, bf16[768,256]{1,0:T(8,128)(2,1)}, u32[]{:S(2)}) %copy-start.2) | copy-done | bytes 393240
  5.4 0.0 copy-start.4
  5.4 1.0 %copy-done.4 = bf16[1024,256]{1,0:T(8,128)(2,1)S(1)} copy-done((bf16[1024,256]{1,0:T(8,128)(2,1)S(1)}, bf16[1024,256]{1,0:T(8,128)(2,1)}, u32[]{:S(2)}) %copy-start.4) | copy-done | bytes 524312
  6.4 0.0 copy-start.10
  6.4 23.3 %user_total.1 = f32[4,256,256]{2,1,0:T(8,128)S(1)} custom-call(s32[8]{0:T(128)S(1)} %bitcast.27, s32[8]{0:T(128)S(1)} %bitcast.29, s32[1]{0:T(128)} %bitcast.17.tile_count, bf16[8,256,256]{2,1,0:T(8,128)(2,1)S(1)} %bitcast.19, bf16[8,256,256]{2,1,0:T(8,128)(2,1)S(1)} %bitcast.21, bf16[4,256,256]{2,1,0:T(8,128)(2,1)S(1)} %bitcast.25, ...), custom_call_target="tpu_custom_call" | custom-call | tf_op jit(solution)/shard_map/user_total/pallas_call | solution.py:403
  29.7 0.0 copy-start.5
  29.7 0.0 copy-start.9
  29.7 0.1 broadcast_multiply_fusion
  29.8 0.0 copy-done.10
  29.8 0.9 %copy-done.5 = bf16[1024,256]{1,0:T(8,128)(2,1)S(1)} copy-done((bf16[1024,256]{1,0:T(8,128)(2,1)S(1)}, bf16[1024,256]{1,0:T(8,128)(2,1)}, u32[]{:S(2)}) %copy-start.5) | copy-done | bytes 524312
  30.8 0.3 copy-done.9
  31.1 0.0 copy-start.3
  31.1 2.8 %select_convert_fusion = (bf16[1024,256]{1,0:T(8,128)(2,1)S(1)}, f32[1024,256]{1,0:T(8,128)}, f32[1024,256]{1,0:T(8,128)}) fusion(bf16[1024,256]{1,0:T(8,128)(2,1)S(1)} %copy-done.5, f32[1024,256]{1,0:T(8,128)S(1)} %copy-done.9, f32[1024,256]{1,0:T(8,128)S(1)} %copy-done.10, f32[4,256,256]{2,1,0:T(8,128)S(1)} %broadcast_multiply_fusion), kind=kLoop, calls=%fused_computation.4 | loop fusion | flops 5242880 | bytes 6291456 | tf_op jit(solution)/shard_map/convert_element_type | solution.py:32
  33.9 0.0 copy-start.6
  33.9 0.0 copy-done.3
  33.9 0.0 copy-start.11
  33.9 0.0 copy-start.12
  33.9 49.1 %item_total.1 = f32[768,256]{1,0:T(8,128)S(1)} custom-call(s32[8]{0:T(128)S(1)} %bitcast.28, s32[8]{0:T(128)S(1)} %bitcast.30, s32[1]{0:T(128)} %bitcast.18.tile_count, bf16[8,256,256]{2,1,0:T(8,128)(2,1)S(1)} %bitcast.20, bf16[8,256,256]{2,1,0:T(8,128)(2,1)S(1)} %bitcast.22, bf16[4,256,256]{2,1,0:T(8,128)(2,1)S(1)} %bitcast.26, ...), custom_call_target="tpu_custom_call" | custom-call | tf_op jit(solution)/shard_map/item_total/pallas_call | solution.py:430
  83.0 0.0 copy-done.6
  83.0 0.0 copy-done.11
  83.1 0.0 copy-done.12
  83.1 1.9 %select_convert_fusion.1 = (bf16[768,256]{1,0:T(8,128)(2,1)}, f32[768,256]{1,0:T(8,128)}, f32[768,256]{1,0:T(8,128)}) fusion(bf16[768,256]{1,0:T(8,128)(2,1)S(1)} %copy-done.3, f32[768,256]{1,0:T(8,128)S(1)} %copy-done.11, f32[768,256]{1,0:T(8,128)S(1)} %copy-done.12, f32[768,256]{1,0:T(8,128)S(1)} %item_total.1), kind=kLoop, calls=%fused_computation.6 | loop fusion | flops 4128768 | bytes 4718592 | tf_op jit(solution)/shard_map/convert_element_type | solution.py:32
Async XLA Ops:
  1.3 0.7 copy-start.7
  1.3 0.7 copy-start.8
  2.0 1.2 %copy-start = (bf16[1,1,8,256,256]{4,3,2,1,0:T(8,128)(2,1)S(1)}, bf16[1,1,8,256,256]{4,3,2,1,0:T(8,128)(2,1)}, u32[]{:S(2)}) copy-start(bf16[1,1,8,256,256]{4,3,2,1,0:T(8,128)(2,1)} %param.11) | copy-start | bytes 3145732
  3.2 1.2 %copy-start.1 = (bf16[1,1,8,256,256]{4,3,2,1,0:T(8,128)(2,1)S(1)}, bf16[1,1,8,256,256]{4,3,2,1,0:T(8,128)(2,1)}, u32[]{:S(2)}) copy-start(bf16[1,1,8,256,256]{4,3,2,1,0:T(8,128)(2,1)} %param.12) | copy-start | bytes 3145732
  4.4 1.0 %copy-start.2 = (bf16[768,256]{1,0:T(8,128)(2,1)S(1)}, bf16[768,256]{1,0:T(8,128)(2,1)}, u32[]{:S(2)}) copy-start(bf16[768,256]{1,0:T(8,128)(2,1)} %param.19) | copy-start | bytes 1179652
  5.4 1.0 %copy-start.4 = (bf16[1024,256]{1,0:T(8,128)(2,1)S(1)}, bf16[1024,256]{1,0:T(8,128)(2,1)}, u32[]{:S(2)}) copy-start(bf16[1024,256]{1,0:T(8,128)(2,1)} %param.16) | copy-start | bytes 1572868
  6.4 23.4 %copy-start.10 = (f32[1024,256]{1,0:T(8,128)S(1)}, f32[1024,256]{1,0:T(8,128)}, u32[]{:S(2)}) copy-start(f32[1024,256]{1,0:T(8,128)} %param.17) | copy-start | bytes 3145732
  29.7 1.0 %copy-start.5 = (bf16[1024,256]{1,0:T(8,128)(2,1)S(1)}, bf16[1024,256]{1,0:T(8,128)(2,1)}, u32[]{:S(2)}) copy-start(bf16[1024,256]{1,0:T(8,128)(2,1)} %param.16) | copy-start | bytes 1572868
  29.7 1.4 %copy-start.9 = (f32[1024,256]{1,0:T(8,128)S(1)}, f32[1024,256]{1,0:T(8,128)}, u32[]{:S(2)}) copy-start(f32[1024,256]{1,0:T(8,128)} %param.18) | copy-start | bytes 3145732
  31.1 2.8 %copy-start.3 = (bf16[768,256]{1,0:T(8,128)(2,1)S(1)}, bf16[768,256]{1,0:T(8,128)(2,1)}, u32[]{:S(2)}) copy-start(bf16[768,256]{1,0:T(8,128)(2,1)} %param.19) | copy-start | bytes 1179652
  33.9 49.2 %copy-start.6 = (bf16[1024,256]{1,0:T(8,128)(2,1)}, bf16[1024,256]{1,0:T(8,128)(2,1)S(1)}, u32[]{:S(2)}) copy-start(bf16[1024,256]{1,0:T(8,128)(2,1)S(1)} %get-tuple-element.9) | copy-start | bytes 1572868
  33.9 49.2 %copy-start.11 = (f32[768,256]{1,0:T(8,128)S(1)}, f32[768,256]{1,0:T(8,128)}, u32[]{:S(2)}) copy-start(f32[768,256]{1,0:T(8,128)} %param.21) | copy-start | bytes 2359300
  33.9 49.2 %copy-start.12 = (f32[768,256]{1,0:T(8,128)S(1)}, f32[768,256]{1,0:T(8,128)}, u32[]{:S(2)}) copy-start(f32[768,256]{1,0:T(8,128)} %param.20) | copy-start | bytes 2359300

commit v2 on v1

v2 whole, which is shorter than its diff:
```python
import functools

import jax
import jax.numpy as jnp
from jax import lax
from jax.experimental import pallas as pl
from jax.experimental.pallas import tpu as pltpu
from jax.sharding import PartitionSpec as P

learn_alpha = 0.25
beta_offset = 1.0
lasso_weight = 0.5
ridge_weight = 1.0

ALONG_Z = 12
CORES = 2


def ftrl_state(gradient, linear, squares, factor):
    new_squares = squares + gradient * gradient
    sigma_step = (jnp.sqrt(new_squares) - jnp.sqrt(squares)) / learn_alpha
    new_linear = linear + gradient - sigma_step * factor.astype(jnp.float32)
    return (new_linear, new_squares)


def ftrl_factor(linear, squares):
    shrink = linear - lasso_weight * jnp.sign(linear)
    denominator = (beta_offset + jnp.sqrt(squares)) / learn_alpha + ridge_weight
    weight = jnp.where(
        jnp.abs(linear) <= lasso_weight, jnp.zeros_like(linear), -shrink / denominator
    )
    return weight.astype(jnp.bfloat16)


def slot_table(tile_user, tile_item, item_blocks):
    return [tile_user[t] * item_blocks + tile_item[t] for t in range(tile_user.shape[0])]


def slot_of(codes, count, pair):
    slot = jnp.int32(0)
    live = jnp.int32(0)
    for t, code in enumerate(codes):
        slot = jnp.where(code == pair, t, slot)
        live = jnp.where(code == pair, jnp.where(t < count, 1, 0), live)
    return slot, live.astype(jnp.float32)


def pair_error(user_rows, item_rows, ratings, confidence, live):
    predict = lax.dot_general(
        user_rows, item_rows, (((1,), (1,)), ((), ())), preferred_element_type=jnp.float32
    )
    error = live * confidence.astype(jnp.float32) * (predict - ratings.astype(jnp.float32))
    return error.astype(jnp.bfloat16)


def remote(source, target, send, receive, device):
    return pltpu.make_async_remote_copy(
        src_ref=source,
        dst_ref=target,
        send_sem=send,
        recv_sem=receive,
        device_id=device,
        device_id_type=pl.DeviceIdType.MESH,
    )


def both_kernel(
    along_z,
    user_scale,
    tile_user,
    tile_item,
    tile_count,
    ratings_hbm,
    confidence_hbm,
    linear_hbm,
    squares_hbm,
    user_factor,
    item_factor,
    user_out,
    total,
    ratings,
    confidence,
    linear,
    squares,
    user_part,
    user_sum,
    fresh,
    pass_right,
    pass_left,
    from_left,
    from_right,
    part,
    arrived,
    mine,
    chunk_sum,
    first_in,
    tile_in,
    whole_in,
    load_sem,
    user_send,
    user_recv,
    send_swap,
    recv_swap,
    send_first,
    recv_first,
    send_second,
    recv_second,
    send_tile,
    recv_tile,
    send_chunk,
    recv_chunk,
    send_over,
    recv_over,
):
    user_blocks, width, rank = user_factor.shape
    item_blocks = item_factor.shape[0]
    half = width // 2
    quarter = width // 4
    half_rows = item_blocks * width // CORES
    along_y = lax.axis_size("users") // (along_z * CORES)
    user = lax.axis_index("users")
    core = lax.rem(user, CORES)
    z = lax.rem(user // CORES, along_z)
    y = user // (CORES * along_z)
    partner = {"users": user + 1 - 2 * core}
    n = lax.axis_size("items")
    me = lax.axis_index("items")
    right, left, far = lax.rem(me + 1, n), lax.rem(me + 3, n), lax.rem(me + 2, n)

    def at_y(t):
        return {"users": (t * along_z + z) * CORES + core}

    def at_z(t):
        return {"users": (y * along_z + t) * CORES + core}

    def greet(device):
        pl.semaphore_signal(
            barrier, inc=1, device_id=device, device_id_type=pl.DeviceIdType.MESH
        )

    barrier = pltpu.get_barrier_semaphore()
    loads = [
        pltpu.make_async_copy(ratings_hbm, ratings, load_sem.at[0]),
        pltpu.make_async_copy(confidence_hbm, confidence, load_sem.at[1]),
        pltpu.make_async_copy(linear_hbm, linear, load_sem.at[2]),
        pltpu.make_async_copy(squares_hbm, squares, load_sem.at[3]),
    ]
    loads[0].start()
    loads[1].start()
    greet({"items": left})
    greet({"items": right})
    greet(partner)

    @pl.loop(1, along_y)
    def _(d):
        greet(at_y(lax.rem(y + d, along_y)))

    @pl.loop(1, along_z)
    def _(d):
        greet(at_z(lax.rem(z + d, along_z)))

    codes = slot_table(tile_user, tile_item, item_blocks)
    count = tile_count[0]

    def user_block(k):
        rows = user_factor[k]
        gradient = jnp.zeros((width, rank), jnp.float32)
        for i in range(item_blocks):
            slot, live = slot_of(codes, count, k * item_blocks + i)
            error = pair_error(rows, item_factor[i], ratings[slot], confidence[slot], live)
            gradient += jnp.dot(error, item_factor[i], preferred_element_type=jnp.float32)
        user_part[k] = gradient

    def rows_at(start, size):
        return pl.ds(start, size)

    low, high = rows_at(0, half), rows_at(half, half)
    fours = [rows_at(q * quarter, quarter) for q in range(4)]
    to_right, to_left = {"items": right}, {"items": left}

    def user_copy(j, source, target, device):
        return remote(source, target, user_send.at[j], user_recv.at[j], device)

    far_right = user_copy(0, user_part.at[far, low], pass_right, to_right)
    far_left = user_copy(1, user_part.at[far, high], pass_left, to_left)
    near_right = user_copy(2, user_part.at[right, high], from_left.at[high], to_right)
    near_left = user_copy(3, user_part.at[left, low], from_right.at[low], to_left)
    sums_right = [
        user_copy(4 + q, user_part.at[right, fours[q]], from_left.at[fours[q]], to_right)
        for q in range(2)
    ]
    sums_left = [
        user_copy(4 + q, user_part.at[left, fours[q]], from_right.at[fours[q]], to_left)
        for q in range(2, 4)
    ]
    own_right = [
        user_copy(8 + q, user_sum.at[me, fours[q]], user_sum.at[me, fours[q]], to_right)
        for q in range(4)
    ]
    own_left = [
        user_copy(12 + q, user_sum.at[me, fours[q]], user_sum.at[me, fours[q]], to_left)
        for q in range(4)
    ]
    on_right = [
        user_copy(16 + q, user_sum.at[left, fours[q]], user_sum.at[left, fours[q]], to_right)
        for q in range(2)
    ]
    on_left = [
        user_copy(16 + q, user_sum.at[right, fours[q]], user_sum.at[right, fours[q]], to_left)
        for q in range(2, 4)
    ]

    loads[0].wait()
    loads[1].wait()
    loads[2].start()
    loads[3].start()
    user_block(far)
    pl.semaphore_wait(barrier, along_y + along_z + 1)
    far_right.start()
    far_left.start()
    user_block(right)
    near_right.start()
    user_block(left)
    near_left.start()
    far_right.wait_recv()
    for q in range(2):
        user_part[right, fours[q]] += pass_right[fours[q]]
        sums_right[q].start()
    far_left.wait_recv()
    for q in range(2, 4):
        user_part[left, fours[q]] += pass_left[fours[q - 2]]
        sums_left[q - 2].start()
    user_block(me)

    def own_sum(q):
        user_sum[me, fours[q]] = user_part[me, fours[q]] + (
            from_left[fours[q]] + from_right[fours[q]]
        )

    near_left.wait_recv()
    near_right.wait_recv()
    for q in range(2):
        sums_right[q].wait_recv()
        own_sum(q)
        own_right[q].start()
        sums_left[q].wait_recv()
        own_sum(2 + q)
        own_left[2 + q].start()
    for q in range(2):
        own_right[2 + q].start()
        own_left[q].start()
    loads[2].wait()
    loads[3].wait()

    def new_factor(k, start):
        slab = min(32, half)

        @pl.loop(0, half // slab)
        def _(j):
            rows = pl.ds(pl.multiple_of(start + j * slab, slab), slab)
            gradient = user_sum[k, rows, :] * user_scale
            state, spread = ftrl_state(
                gradient, linear[k, rows, :], squares[k, rows, :], user_factor[k, rows, :]
            )
            shrink = state - jnp.where(state > 0.0, lasso_weight, -lasso_weight)
            denominator = (beta_offset + jnp.sqrt(spread)) / learn_alpha + ridge_weight
            weight = jnp.where(
                jnp.abs(state) <= lasso_weight, jnp.zeros_like(state), -shrink / denominator
            )
            fresh[k, rows, :] = weight.astype(jnp.bfloat16)

    def item_block(k, i, first=False):
        rows = pl.ds(pl.multiple_of(i * width, width), width)
        slot, live = slot_of(codes, count, k * item_blocks + i)
        error = pair_error(fresh[k], item_factor[i], ratings[slot], confidence[slot], live)
        gradient = lax.dot_general(
            error, fresh[k], (((0,), (0,)), ((), ())), preferred_element_type=jnp.float32
        )
        if first:
            part[rows, :] = gradient
        else:
            part[rows, :] += gradient

    new_factor(me, 0)
    new_factor(me, half)
    for q in range(2):
        own_right[q].wait_recv()
        on_right[q].start()
        own_left[2 + q].wait_recv()
        on_left[q].start()
    for i in range(item_blocks):
        item_block(me, i, first=True)
    new_factor(left, 0)
    new_factor(right, half)
    own_right[2].wait_recv()
    own_right[3].wait_recv()
    new_factor(left, half)
    for i in range(item_blocks):
        item_block(left, i)
    own_left[0].wait_recv()
    own_left[1].wait_recv()
    new_factor(right, 0)
    for i in range(item_blocks):
        item_block(right, i)
    for copy in on_right:
        copy.wait_recv()
    new_factor(far, 0)
    for copy in on_left:
        copy.wait_recv()
    new_factor(far, half)
    store = pltpu.make_async_copy(user_sum, user_out, load_sem.at[4])
    store.start()
    item_block(far, (item_blocks - 1) * (1 - core))
    item_block(far, 1)

    def distance(count, j):
        step = (j + 1) // 2
        return count // 2 + step * (1 - 2 * lax.rem(j, 2))

    def swaps(base, count, place):
        chunk = half_rows // count

        def one(j):
            t = lax.rem(place + distance(count, j), count)
            return remote(
                part.at[pl.ds(pl.multiple_of(base + t * chunk, 8), chunk)],
                arrived.at[pl.ds(pl.multiple_of(t * chunk, 8), chunk)],
                send_swap.at[j],
                recv_swap.at[j],
                partner,
            )

        return one

    def halves(other, base, n_first, first, at_first, n_second, second, at_second, direct):
        chunk = half_rows // n_first
        to_partner = swaps(other, n_second, second)
        from_partner = swaps(base, n_first, first)

        @pl.loop(0, n_second)
        def _(j):
            to_partner(j).start()

        item_block(far, (item_blocks - 1) * (base // half_rows))

        def rows_of(t):
            return pl.ds(pl.multiple_of(t * chunk, 8), chunk)

        def out_rows(t):
            return pl.ds(pl.multiple_of(base + t * chunk, 8), chunk)

        def tile_of(t, start):
            return (
                pl.ds(pl.multiple_of(start + 8 * (t // 2), 8), 8),
                pl.ds(pl.multiple_of(128 * lax.rem(t, 2), 128), 128),
            )

        def first_target(j):
            return lax.rem(first + distance(n_first, j), n_first)

        def second_target(j):
            return lax.rem(second + distance(n_second, j), n_second)

        def to_first(j):
            t = first_target(j)
            return remote(
                mine.at[rows_of(t)],
                first_in.at[j, pl.ds(0, chunk)],
                send_first.at[j],
                recv_first.at[j],
                at_first(t),
            )

        def to_second(j):
            t = second_target(j)
            return remote(
                chunk_sum.at[tile_of(t, 0)],
                tile_in.at[j],
                send_second.at[j],
                recv_second.at[j],
                at_second(t),
            )

        def whole_to(j):
            return remote(
                whole_in.at[second],
                whole_in.at[second],
                send_second.at[j],
                recv_second.at[j],
                at_second(second_target(j)),
            )

        my_tile = tile_of(second, base + first * chunk)

        def tile_out(j):
            return remote(
                total.at[my_tile],
                total.at[my_tile],
                send_tile.at[j],
                recv_tile.at[j],
                at_second(second_target(j)),
            )

        def chunk_out(j):
            return remote(
                total.at[out_rows(first)],
                total.at[out_rows(first)],
                send_chunk.at[j],
                recv_chunk.at[j],
                at_first(first_target(j)),
            )

        def over(slot, t):
            return remote(
                total.at[out_rows(t)],
                total.at[out_rows(t)],
                send_over.at[slot],
                recv_over.at[slot],
                partner,
            )

        @pl.loop(0, n_first - 1)
        def _(j):
            t = first_target(j)
            from_partner(j).wait_recv()
            mine[rows_of(t), :] = part[out_rows(t), :] + arrived[rows_of(t), :]
            to_first(j).start()

        from_partner(n_first - 1).wait_recv()

        def add_first(j, running):
            to_first(j).wait_recv()
            return running + first_in[j, pl.ds(0, chunk), :]

        near = lax.fori_loop(
            0,
            n_first - 1,
            add_first,
            part[out_rows(first), :] + arrived[rows_of(first), :],
        )

        if direct:
            whole_in[second] = near

            @pl.loop(0, n_second - 1)
            def _(j):
                whole_to(j).start()

            @pl.loop(0, n_second - 1)
            def _(j):
                whole_to(j).wait_recv()

            total[out_rows(first), :] = lax.fori_loop(
                1, n_second, lambda j, running: running + whole_in[j], whole_in[0]
            )
        else:
            chunk_sum[...] = near

            @pl.loop(0, n_second - 1)
            def _(j):
                to_second(j).start()

            def add_second(j, running):
                to_second(j).wait_recv()
                return running + tile_in[j]

            total[my_tile] = lax.fori_loop(
                0, n_second - 1, add_second, chunk_sum[tile_of(second, 0)]
            )

            @pl.loop(0, n_second - 1)
            def _(j):
                tile_out(j).start()

            @pl.loop(0, n_second - 1)
            def _(j):
                tile_out(j).wait_recv()

        @pl.loop(0, n_first - 1)
        def _(j):
            chunk_out(j).start()

        over(n_first - 1, first).start()

        @pl.loop(0, n_first - 1)
        def _(j):
            chunk_out(j).wait_recv()
            over(j, lax.rem(first + n_first - distance(n_first, j), n_first)).start()

        @pl.loop(0, n_first - 1)
        def _(j):
            to_first(j).wait_send()
            chunk_out(j).wait_send()

        @pl.loop(0, n_second - 1)
        def _(j):
            if direct:
                whole_to(j).wait_send()
            else:
                to_second(j).wait_send()
                tile_out(j).wait_send()

        @pl.loop(0, n_first)
        def _(j):
            over(j, 0).wait_send()

        @pl.loop(0, n_second)
        def _(j):
            to_partner(j).wait_send()

        other_chunk = half_rows // n_second

        @pl.loop(0, n_second)
        def _(j):
            remote(
                total.at[pl.ds(0, other_chunk)],
                total.at[pl.ds(0, other_chunk)],
                send_over.at[j],
                recv_over.at[j],
                partner,
            ).wait_recv()

    @pl.when(core == 0)
    def _():
        halves(half_rows, 0, along_y, y, at_y, along_z, z, at_z, False)

    @pl.when(core == 1)
    def _():
        halves(0, half_rows, along_z, z, at_z, along_y, y, at_y, True)

    for copy in [far_right, far_left, near_right, near_left] + sums_right + sums_left:
        copy.wait_send()
    for copy in own_right + own_left + on_right + on_left:
        copy.wait_send()
    store.wait()


VMEM = pl.BlockSpec(memory_space=pltpu.VMEM)
SMEM = pl.BlockSpec(memory_space=pltpu.SMEM)
ANY = pl.BlockSpec(memory_space=pl.ANY)
DMA = pltpu.SemaphoreType.DMA


def both_totals(tiles, linear, squares, user_factor, item_factor, along_y, along_z):
    blocks, width, rank = user_factor.shape
    rows = item_factor.shape[0] * width
    half_rows = rows // CORES
    most = max(along_y, along_z)
    chunk_y, chunk_z = half_rows // along_y, half_rows // along_z
    chunk = max(chunk_y, chunk_z)
    f32 = jnp.float32
    whole = (blocks, width, rank)
    return pl.pallas_call(
        functools.partial(both_kernel, along_z, width ** (-0.5)),
        name="both_totals",
        out_shape=(jax.ShapeDtypeStruct(whole, f32), jax.ShapeDtypeStruct((rows, rank), f32)),
        in_specs=[SMEM] * 3 + [ANY] * 4 + [VMEM] * 2,
        out_specs=(ANY, VMEM),
        scratch_shapes=[
            pltpu.VMEM(tiles[3].shape, tiles[3].dtype),
            pltpu.VMEM(tiles[4].shape, tiles[4].dtype),
            pltpu.VMEM(whole, f32),
            pltpu.VMEM(whole, f32),
            pltpu.VMEM(whole, f32),
            pltpu.VMEM(whole, f32),
            pltpu.VMEM(whole, user_factor.dtype),
            pltpu.VMEM((width // 2, rank), f32),
            pltpu.VMEM((width // 2, rank), f32),
            pltpu.VMEM((width, rank), f32),
            pltpu.VMEM((width, rank), f32),
            pltpu.VMEM((rows, rank), f32),
            pltpu.VMEM((half_rows, rank), f32),
            pltpu.VMEM((half_rows, rank), f32),
            pltpu.VMEM((chunk_y, rank), f32),
            pltpu.VMEM((most - 1, chunk, rank), f32),
            pltpu.VMEM((most - 1, 8, 128), f32),
            pltpu.VMEM((along_y, chunk_z, rank), f32),
            DMA((5,)),
            DMA((20,)),
            DMA((20,)),
        ]
        + [DMA((most,))] * 12,
        compiler_params=pltpu.CompilerParams(collective_id=0, has_side_effects=True),
    )(*tiles, linear, squares, user_factor, item_factor)


def on_device(
    ratings,
    confidence,
    tile_user,
    tile_item,
    tile_count,
    user_factor,
    user_linear,
    user_squares,
    item_factor,
    item_linear,
    item_squares,
):
    slot_count = ratings.shape[2]
    width = ratings.shape[3]
    rank = user_factor.shape[1]
    user_blocks = user_factor.shape[0] // width
    item_blocks = item_factor.shape[0] // width
    user_devices = lax.axis_size("users")
    tiles = (
        tile_user.reshape(slot_count),
        tile_item.reshape(slot_count),
        tile_count.reshape(1),
        ratings.reshape(slot_count, width, width),
        confidence.reshape(slot_count, width, width),
    )
    items = item_factor.reshape(item_blocks, width, rank)
    split = (user_blocks, width, rank)
    user_sum, item_sum = both_totals(
        tiles,
        user_linear.reshape(split),
        user_squares.reshape(split),
        user_factor.reshape(split),
        items,
        user_devices // (ALONG_Z * CORES),
        ALONG_Z,
    )
    user_grad = user_sum.reshape(user_blocks * width, rank) * width ** (-0.5)
    new_user_linear, new_user_squares = ftrl_state(
        user_grad, user_linear, user_squares, user_factor
    )
    new_user_factor = ftrl_factor(new_user_linear, new_user_squares)
    item_grad = item_sum * (width * user_devices) ** (-0.5)
    new_item_linear, new_item_squares = ftrl_state(
        item_grad, item_linear, item_squares, item_factor
    )
    new_item_factor = ftrl_factor(new_item_linear, new_item_squares)
    return (
        new_user_factor,
        new_user_linear,
        new_user_squares,
        new_item_factor,
        new_item_linear,
        new_item_squares,
    )


def solution(mesh):
    placed = (
        P("users", "items", None, None, None),
        P("users", "items", None, None, None),
        P("users", "items", None),
        P("users", "items", None),
        P("users", "items"),
        P("users", None),
        P("users", None),
        P("users", None),
        P("items", None),
        P("items", None),
        P("items", None),
    )
    return jax.shard_map(
        on_device,
        mesh=mesh,
        in_specs=placed,
        out_specs=(
            P("users", None),
            P("users", None),
            P("users", None),
            P("items", None),
            P("items", None),
            P("items", None),
        ),
        check_vma=False,
    )
```

time: 85.3 us -> 81.1 us (0.951)
  local copies, waits for them, and re-layouts: 6.44 us -> 0.38 us
  Pallas kernels: 72.4 us -> 73.6 us
  other arithmetic: 4.72 us -> 5.61 us
    unnamed x26 -> x14, local copies, waits for them, and re-layouts: 6.44 us -> 0.38 us
    mul x1, other arithmetic: 0.08 us -> 1.47 us  [on_device(): user_grad = user_sum.reshape(user_blocks * width, rank) * width ** (-0.5)]
    pallas_call x2 -> x1, Pallas kernels: 72.4 us -> 73.6 us  [both_totals(): pl.pallas_call(functools.partial(both_kernel, along_z, width ** (-0.5)),...]
where the time goes in v2:
time: 81.1 us; the launch traced here: 80.9 us
  Pallas kernels  73.6 us (91%)
  other arithmetic  5.61 us (7%)
  between operations  1.35 us (2%)
    pallas_call x1, Pallas kernels, both_totals(): pl.pallas_call(functools.partial(both_kernel, along_z, width ** (-0.5)),...  73.6 us
    convert_element_type x2, other arithmetic, ftrl_factor(): return weight.astype(jnp.bfloat16)  4.14 us

profile of v2, /device:TPU:1, one launch (start us, length us, event | category | flops | bytes accessed | tf_op | source)
XLA Modules:
  0.0 80.9 jit_solution(1400599444709996483)
XLA Ops:
  1.3 0.0 copy-start.2
  1.3 73.6 %both_totals.1 = (f32[4,256,256]{2,1,0:T(8,128)}, f32[768,256]{1,0:T(8,128)}) custom-call(s32[8]{0:T(128)} %bitcast.25, s32[8]{0:T(128)} %bitcast.26, s32[1]{0:T(128)} %bitcast.18.tile_count, bf16[8,256,256]{2,1,0:T(8,128)(2,1)} %bitcast.23, bf16[8,256,256]{2,1,0:T(8,128)(2,1)} %bitcast.24, f32[4,256,256]{2,1,0:T(8,128)} %bitcast.20, ...), custom_call_target="tpu_custom_call" | custom-call | tf_op jit(solution)/shard_map/both_totals/pallas_call | solution.py:553
  74.9 0.0 copy-start
  74.9 0.0 copy-start.1
  74.9 1.5 %broadcast_multiply_fusion = f32[4,256,256]{2,1,0:T(8,128)S(1)} fusion(f32[4,256,256]{2,1,0:T(8,128)} %get-tuple-element.8), kind=kLoop, calls=%fused_computation.10 | loop fusion | flops 262144 | bytes 2097152 | tf_op jit(solution)/shard_map/mul | solution.py:624
  76.4 0.0 copy-done.2
  76.4 0.0 copy-done
  76.4 0.3 copy-done.1
  76.8 0.0 copy-start.3
  76.8 0.0 copy-start.4
  76.8 0.0 copy-start.5
  76.8 0.0 copy-start.6
  76.8 2.3 %select_convert_fusion = (bf16[1024,256]{1,0:T(8,128)(2,1)}, f32[1024,256]{1,0:T(8,128)}, f32[1024,256]{1,0:T(8,128)}) fusion(bf16[1024,256]{1,0:T(8,128)(2,1)S(1)} %copy-done.2, f32[1024,256]{1,0:T(8,128)S(1)} %copy-done, f32[1024,256]{1,0:T(8,128)S(1)} %copy-done.1, f32[4,256,256]{2,1,0:T(8,128)S(1)} %broadcast_multiply_fusion), kind=kLoop, calls=%fused_computation.4 | loop fusion | flops 5242880 | bytes 6291456 | tf_op jit(solution)/shard_map/convert_element_type | solution.py:32
  79.0 0.0 copy-done.3
  79.0 0.0 copy-done.4
  79.0 0.0 copy-done.5
  79.0 0.0 copy-done.6
  79.1 1.9 %select_convert_fusion.1 = (bf16[768,256]{1,0:T(8,128)(2,1)}, f32[768,256]{1,0:T(8,128)}, f32[768,256]{1,0:T(8,128)}) fusion(bf16[768,256]{1,0:T(8,128)(2,1)S(1)} %copy-done.3, f32[768,256]{1,0:T(8,128)S(1)} %copy-done.4, f32[768,256]{1,0:T(8,128)S(1)} %copy-done.5, f32[768,256]{1,0:T(8,128)S(1)} %copy-done.6), kind=kLoop, calls=%fused_computation.6 | loop fusion | flops 4128768 | bytes 4718592 | tf_op jit(solution)/shard_map/convert_element_type | solution.py:32
Async XLA Ops:
  1.3 75.1 %copy-start.2 = (bf16[1024,256]{1,0:T(8,128)(2,1)S(1)}, bf16[1024,256]{1,0:T(8,128)(2,1)}, u32[]{:S(2)}) copy-start(bf16[1024,256]{1,0:T(8,128)(2,1)} %param.16) | copy-start | bytes 1572868
  74.9 1.5 %copy-start = (f32[1024,256]{1,0:T(8,128)S(1)}, f32[1024,256]{1,0:T(8,128)}, u32[]{:S(2)}) copy-start(f32[1024,256]{1,0:T(8,128)} %param.18) | copy-start | bytes 3145732
  74.9 1.8 %copy-start.1 = (f32[1024,256]{1,0:T(8,128)S(1)}, f32[1024,256]{1,0:T(8,128)}, u32[]{:S(2)}) copy-start(f32[1024,256]{1,0:T(8,128)} %param.17) | copy-start | bytes 3145732
  76.8 2.3 %copy-start.3 = (bf16[768,256]{1,0:T(8,128)(2,1)S(1)}, bf16[768,256]{1,0:T(8,128)(2,1)}, u32[]{:S(2)}) copy-start(bf16[768,256]{1,0:T(8,128)(2,1)} %param.19) | copy-start | bytes 1179652
  76.8 2.3 %copy-start.4 = (f32[768,256]{1,0:T(8,128)S(1)}, f32[768,256]{1,0:T(8,128)}, u32[]{:S(2)}) copy-start(f32[768,256]{1,0:T(8,128)} %param.21) | copy-start | bytes 2359300
  76.8 2.3 %copy-start.5 = (f32[768,256]{1,0:T(8,128)S(1)}, f32[768,256]{1,0:T(8,128)}, u32[]{:S(2)}) copy-start(f32[768,256]{1,0:T(8,128)} %param.20) | copy-start | bytes 2359300
  76.8 2.3 %copy-start.6 = (f32[768,256]{1,0:T(8,128)S(1)}, f32[768,256]{1,0:T(8,128)}, u32[]{:S(2)}) copy-start(f32[768,256]{1,0:T(8,128)} %get-tuple-element.9) | copy-start | bytes 2359300

commit v3 on v2

--- a/solution.py
+++ b/solution.py
@@ -233,8 +233,8 @@
     user_block(me)
 
     def own_sum(q):
-        user_sum[me, fours[q]] = user_part[me, fours[q]] + (
-            from_left[fours[q]] + from_right[fours[q]]
+        user_sum[me, fours[q]] = user_scale * (
+            user_part[me, fours[q]] + (from_left[fours[q]] + from_right[fours[q]])
         )
 
     near_left.wait_recv()
@@ -258,9 +258,8 @@
         @pl.loop(0, half // slab)
         def _(j):
             rows = pl.ds(pl.multiple_of(start + j * slab, slab), slab)
-            gradient = user_sum[k, rows, :] * user_scale
             state, spread = ftrl_state(
-                gradient, linear[k, rows, :], squares[k, rows, :], user_factor[k, rows, :]
+                user_sum[k, rows, :], linear[k, rows, :], squares[k, rows, :], user_factor[k, rows, :]
             )
             shrink = state - jnp.where(state > 0.0, lasso_weight, -lasso_weight)
             denominator = (beta_offset + jnp.sqrt(spread)) / learn_alpha + ridge_weight
@@ -317,11 +316,28 @@
         step = (j + 1) // 2
         return count // 2 + step * (1 - 2 * lax.rem(j, 2))
 
+    def shifted(count, place, offset):
+        return lax.rem(place + offset + count, count)
+
+    def chunk_offset(count, j):
+        reach = count // 4
+        q = j - (2 * reach - 1)
+        near = (1 + q // 2) * (2 * lax.rem(q + 2 * reach, 2) - 1)
+        return jnp.where(
+            j < reach,
+            j - 2 * reach,
+            jnp.where(
+                j < 2 * reach - 1,
+                3 * reach - 1 - j,
+                jnp.where(j < count - 1, near, 0),
+            ),
+        )
+
     def swaps(base, count, place):
         chunk = half_rows // count
 
         def one(j):
-            t = lax.rem(place + distance(count, j), count)
+            t = shifted(count, place, chunk_offset(count, j))
             return remote(
                 part.at[pl.ds(pl.multiple_of(base + t * chunk, 8), chunk)],
                 arrived.at[pl.ds(pl.multiple_of(t * chunk, 8), chunk)],
@@ -355,20 +371,27 @@
                 pl.ds(pl.multiple_of(128 * lax.rem(t, 2), 128), 128),
             )
 
-        def first_target(j):
-            return lax.rem(first + distance(n_first, j), n_first)
+        reach = n_first // 4
+
+        def chunk_at(offset):
+            return shifted(n_first, first, offset)
 
         def second_target(j):
             return lax.rem(second + distance(n_second, j), n_second)
 
         def to_first(j):
-            t = first_target(j)
+            offset = chunk_offset(n_first, j)
+            hop = jnp.where(
+                j < reach,
+                j - reach,
+                jnp.where(j < 2 * reach - 1, 2 * reach - 1 - j, offset),
+            )
             return remote(
-                mine.at[rows_of(t)],
+                mine.at[rows_of(chunk_at(offset))],
                 first_in.at[j, pl.ds(0, chunk)],
                 send_first.at[j],
                 recv_first.at[j],
-                at_first(t),
+                at_first(chunk_at(hop)),
             )
 
         def to_second(j):
@@ -401,14 +424,27 @@
                 at_second(second_target(j)),
             )
 
-        def chunk_out(j):
+        def spread(slot, owner, hop):
+            rows = out_rows(chunk_at(owner))
             return remote(
-                total.at[out_rows(first)],
-                total.at[out_rows(first)],
-                send_chunk.at[j],
-                recv_chunk.at[j],
-                at_first(first_target(j)),
-            )
+                total.at[rows],
+                total.at[rows],
+                send_chunk.at[slot],
+                recv_chunk.at[slot],
+                at_first(chunk_at(hop)),
+            )
+
+        def near_hop(j):
+            return (reach - j // 2) * (2 * lax.rem(j, 2) - 1)
+
+        def near_out(j):
+            return spread(j, 0, near_hop(j))
+
+        def on_down(j):
+            return spread(2 * reach + j, reach, j - reach)
+
+        def on_up(j):
+            return spread(3 * reach + j, -reach, reach - 1 - j)
 
         def over(slot, t):
             return remote(
@@ -419,25 +455,28 @@
                 partner,
             )
 
-        @pl.loop(0, n_first - 1)
-        def _(j):
-            t = first_target(j)
+        def swapped(j):
             from_partner(j).wait_recv()
-            mine[rows_of(t), :] = part[out_rows(t), :] + arrived[rows_of(t), :]
+            t = chunk_at(chunk_offset(n_first, j))
+            return part[out_rows(t), :] + arrived[rows_of(t), :]
+
+        @pl.loop(0, n_first - 3)
+        def _(j):
+            mine[rows_of(chunk_at(chunk_offset(n_first, j))), :] = swapped(j)
             to_first(j).start()
-
-        from_partner(n_first - 1).wait_recv()
 
         def add_first(j, running):
             to_first(j).wait_recv()
             return running + first_in[j, pl.ds(0, chunk), :]
 
-        near = lax.fori_loop(
-            0,
-            n_first - 1,
-            add_first,
-            part[out_rows(first), :] + arrived[rows_of(first), :],
+        down, up = n_first - 3, n_first - 2
+        mine[rows_of(chunk_at(-reach)), :] = lax.fori_loop(0, reach, add_first, swapped(down))
+        to_first(down).start()
+        mine[rows_of(chunk_at(reach)), :] = lax.fori_loop(
+            reach, 2 * reach - 1, add_first, swapped(up)
         )
+        to_first(up).start()
+        near = lax.fori_loop(2 * reach - 1, n_first - 1, add_first, swapped(n_first - 1))
 
         if direct:
             whole_in[second] = near
@@ -476,21 +515,57 @@
             def _(j):
                 tile_out(j).wait_recv()
 
+        @pl.loop(0, 2 * reach)
+        def _(j):
+            near_out(j).start()
+
+        over(n_first - 1, first).start()
+
+        near_out(0).wait_recv()
+
+        @pl.loop(0, reach)
+        def _(j):
+            on_down(j).start()
+
+        near_out(1).wait_recv()
+
+        @pl.loop(0, reach - 1)
+        def _(j):
+            on_up(j).start()
+
+        over(0, chunk_at(reach)).start()
+        over(1, chunk_at(-reach)).start()
+
+        @pl.loop(2, 2 * reach)
+        def _(j):
+            near_out(j).wait_recv()
+            over(j, chunk_at(-near_hop(j))).start()
+
+        @pl.loop(0, reach)
+        def _(j):
+            on_down(j).wait_recv()
+            over(2 * reach + j, chunk_at(2 * reach - j)).start()
+
+        @pl.loop(0, reach - 1)
+        def _(j):
+            on_up(j).wait_recv()
+            over(3 * reach + j, chunk_at(1 + j - 2 * reach)).start()
+
         @pl.loop(0, n_first - 1)
         def _(j):
-            chunk_out(j).start()
-
-        over(n_first - 1, first).start()
-
-        @pl.loop(0, n_first - 1)
-        def _(j):
-            chunk_out(j).wait_recv()
-            over(j, lax.rem(first + n_first - distance(n_first, j), n_first)).start()
-
-        @pl.loop(0, n_first - 1)
-        def _(j):
             to_first(j).wait_send()
-            chunk_out(j).wait_send()
+
+        @pl.loop(0, 2 * reach)
+        def _(j):
+            near_out(j).wait_send()
+
+        @pl.loop(0, reach)
+        def _(j):
+            on_down(j).wait_send()
+
+        @pl.loop(0, reach - 1)
+        def _(j):
+            on_up(j).wait_send()
 
         @pl.loop(0, n_second - 1)
         def _(j):
@@ -621,7 +696,7 @@
         user_devices // (ALONG_Z * CORES),
         ALONG_Z,
     )
-    user_grad = user_sum.reshape(user_blocks * width, rank) * width ** (-0.5)
+    user_grad = user_sum.reshape(user_blocks * width, rank)
     new_user_linear, new_user_squares = ftrl_state(
         user_grad, user_linear, user_squares, user_factor
     )

time: 81.1 us -> 82.2 us (1.014)
  Pallas kernels: 73.6 us -> 75.1 us
    pallas_call x1, Pallas kernels: 73.6 us -> 75.1 us  [both_totals(): pl.pallas_call(functools.partial(both_kernel, along_z, width ** (-0.5)),...]
    mul x1 -> x0, other arithmetic: 1.47 us -> none  [on_device(): user_grad = user_sum.reshape(user_blocks * width, rank) * width ** (-0.5)]
    convert_element_type x2, other arithmetic: 4.14 us -> 5.49 us  [ftrl_factor(): return weight.astype(jnp.bfloat16)]
where the time goes in v3:
time: 82.2 us; the launch traced here: 82 us
  Pallas kernels  75.1 us (91%)
  other arithmetic  5.49 us (7%)
  between operations  1.38 us (2%)
    pallas_call x1, Pallas kernels, both_totals(): pl.pallas_call(functools.partial(both_kernel, along_z, width ** (-0.5)),...  75.1 us
    convert_element_type x2, other arithmetic, ftrl_factor(): return weight.astype(jnp.bfloat16)  5.49 us

profile of v3, /device:TPU:1, one launch (start us, length us, event | category | flops | bytes accessed | tf_op | source)
XLA Modules:
  0.0 82.0 jit_solution(1296187063644598404)
XLA Ops:
  1.3 0.0 copy-start
  1.3 0.0 copy-start.1
  1.3 0.0 copy-start.2
  1.3 75.1 %both_totals.1 = (f32[4,256,256]{2,1,0:T(8,128)}, f32[768,256]{1,0:T(8,128)}) custom-call(s32[8]{0:T(128)} %bitcast.25, s32[8]{0:T(128)} %bitcast.26, s32[1]{0:T(128)} %bitcast.18.tile_count, bf16[8,256,256]{2,1,0:T(8,128)(2,1)} %bitcast.23, bf16[8,256,256]{2,1,0:T(8,128)(2,1)} %bitcast.24, f32[4,256,256]{2,1,0:T(8,128)} %bitcast.20, ...), custom_call_target="tpu_custom_call" | custom-call | tf_op jit(solution)/shard_map/both_totals/pallas_call | solution.py:628
  76.4 0.0 copy-done
  76.4 0.0 copy-done.1
  76.5 0.0 copy-done.2
  76.5 0.0 copy-start.3
  76.5 0.0 copy-start.4
  76.5 0.0 copy-start.5
  76.5 0.0 copy-start.6
  76.5 3.6 %select_convert_fusion = (bf16[1024,256]{1,0:T(8,128)(2,1)}, f32[1024,256]{1,0:T(8,128)}, f32[1024,256]{1,0:T(8,128)}) fusion(bf16[1024,256]{1,0:T(8,128)(2,1)S(1)} %copy-done.2, f32[1024,256]{1,0:T(8,128)S(1)} %copy-done, f32[1024,256]{1,0:T(8,128)S(1)} %copy-done.1, f32[4,256,256]{2,1,0:T(8,128)} %get-tuple-element.8), kind=kLoop, calls=%fused_computation.4 | loop fusion | flops 5242880 | bytes 6291456 | tf_op jit(solution)/shard_map/convert_element_type | solution.py:32
  80.1 0.0 copy-done.3
  80.1 0.0 copy-done.4
  80.1 0.0 copy-done.5
  80.1 0.0 copy-done.6
  80.1 1.9 %select_convert_fusion.1 = (bf16[768,256]{1,0:T(8,128)(2,1)}, f32[768,256]{1,0:T(8,128)}, f32[768,256]{1,0:T(8,128)}) fusion(bf16[768,256]{1,0:T(8,128)(2,1)S(1)} %copy-done.3, f32[768,256]{1,0:T(8,128)S(1)} %copy-done.4, f32[768,256]{1,0:T(8,128)S(1)} %copy-done.5, f32[768,256]{1,0:T(8,128)S(1)} %copy-done.6), kind=kLoop, calls=%fused_computation.6 | loop fusion | flops 4128768 | bytes 4718592 | tf_op jit(solution)/shard_map/convert_element_type | solution.py:32
Async XLA Ops:
  1.3 75.2 %copy-start = (f32[1024,256]{1,0:T(8,128)S(1)}, f32[1024,256]{1,0:T(8,128)}, u32[]{:S(2)}) copy-start(f32[1024,256]{1,0:T(8,128)} %param.18) | copy-start | bytes 3145732
  1.3 75.2 %copy-start.1 = (f32[1024,256]{1,0:T(8,128)S(1)}, f32[1024,256]{1,0:T(8,128)}, u32[]{:S(2)}) copy-start(f32[1024,256]{1,0:T(8,128)} %param.17) | copy-start | bytes 3145732
  1.3 75.2 %copy-start.2 = (bf16[1024,256]{1,0:T(8,128)(2,1)S(1)}, bf16[1024,256]{1,0:T(8,128)(2,1)}, u32[]{:S(2)}) copy-start(bf16[1024,256]{1,0:T(8,128)(2,1)} %param.16) | copy-start | bytes 1572868
  76.5 3.7 %copy-start.3 = (bf16[768,256]{1,0:T(8,128)(2,1)S(1)}, bf16[768,256]{1,0:T(8,128)(2,1)}, u32[]{:S(2)}) copy-start(bf16[768,256]{1,0:T(8,128)(2,1)} %param.19) | copy-start | bytes 1179652
  76.5 3.6 %copy-start.4 = (f32[768,256]{1,0:T(8,128)S(1)}, f32[768,256]{1,0:T(8,128)}, u32[]{:S(2)}) copy-start(f32[768,256]{1,0:T(8,128)} %param.21) | copy-start | bytes 2359300
  76.5 3.6 %copy-start.5 = (f32[768,256]{1,0:T(8,128)S(1)}, f32[768,256]{1,0:T(8,128)}, u32[]{:S(2)}) copy-start(f32[768,256]{1,0:T(8,128)} %param.20) | copy-start | bytes 2359300
  76.5 3.6 %copy-start.6 = (f32[768,256]{1,0:T(8,128)S(1)}, f32[768,256]{1,0:T(8,128)}, u32[]{:S(2)}) copy-start(f32[768,256]{1,0:T(8,128)} %get-tuple-element.9) | copy-start | bytes 2359300

commit v4 on v2

--- a/solution.py
+++ b/solution.py
@@ -233,8 +233,8 @@
     user_block(me)
 
     def own_sum(q):
-        user_sum[me, fours[q]] = user_part[me, fours[q]] + (
-            from_left[fours[q]] + from_right[fours[q]]
+        user_sum[me, fours[q]] = user_scale * (
+            user_part[me, fours[q]] + (from_left[fours[q]] + from_right[fours[q]])
         )
 
     near_left.wait_recv()
@@ -258,9 +258,8 @@
         @pl.loop(0, half // slab)
         def _(j):
             rows = pl.ds(pl.multiple_of(start + j * slab, slab), slab)
-            gradient = user_sum[k, rows, :] * user_scale
             state, spread = ftrl_state(
-                gradient, linear[k, rows, :], squares[k, rows, :], user_factor[k, rows, :]
+                user_sum[k, rows, :], linear[k, rows, :], squares[k, rows, :], user_factor[k, rows, :]
             )
             shrink = state - jnp.where(state > 0.0, lasso_weight, -lasso_weight)
             denominator = (beta_offset + jnp.sqrt(spread)) / learn_alpha + ridge_weight
@@ -361,13 +360,16 @@
         def second_target(j):
             return lax.rem(second + distance(n_second, j), n_second)
 
-        def to_first(j):
+        columns = [pl.ds(0, rank // 2), pl.ds(rank // 2, rank // 2)]
+        most = first_in.shape[0]
+
+        def to_first(h, j):
             t = first_target(j)
             return remote(
-                mine.at[rows_of(t)],
-                first_in.at[j, pl.ds(0, chunk)],
-                send_first.at[j],
-                recv_first.at[j],
+                mine.at[rows_of(t), columns[h]],
+                first_in.at[j, pl.ds(0, chunk), columns[h]],
+                send_first.at[h * most + j],
+                recv_first.at[h * most + j],
                 at_first(t),
             )
 
@@ -381,12 +383,12 @@
                 at_second(t),
             )
 
-        def whole_to(j):
+        def whole_to(h, j):
             return remote(
-                whole_in.at[second],
-                whole_in.at[second],
-                send_second.at[j],
-                recv_second.at[j],
+                whole_in.at[second, :, columns[h]],
+                whole_in.at[second, :, columns[h]],
+                send_second.at[h * most + j],
+                recv_second.at[h * most + j],
                 at_second(second_target(j)),
             )
 
@@ -401,12 +403,12 @@
                 at_second(second_target(j)),
             )
 
-        def chunk_out(j):
+        def chunk_out(h, j):
             return remote(
-                total.at[out_rows(first)],
-                total.at[out_rows(first)],
-                send_chunk.at[j],
-                recv_chunk.at[j],
+                total.at[out_rows(first), columns[h]],
+                total.at[out_rows(first), columns[h]],
+                send_chunk.at[h * most + j],
+                recv_chunk.at[h * most + j],
                 at_first(first_target(j)),
             )
 
@@ -421,44 +423,67 @@
 
         @pl.loop(0, n_first - 1)
         def _(j):
+            from_partner(j).wait_recv()
             t = first_target(j)
-            from_partner(j).wait_recv()
             mine[rows_of(t), :] = part[out_rows(t), :] + arrived[rows_of(t), :]
-            to_first(j).start()
+            to_first(0, j).start()
+
+        @pl.loop(0, n_first - 1)
+        def _(j):
+            to_first(1, j).start()
 
         from_partner(n_first - 1).wait_recv()
 
-        def add_first(j, running):
-            to_first(j).wait_recv()
-            return running + first_in[j, pl.ds(0, chunk), :]
-
-        near = lax.fori_loop(
-            0,
-            n_first - 1,
-            add_first,
-            part[out_rows(first), :] + arrived[rows_of(first), :],
-        )
+        def near(h):
+            def add_first(j, running):
+                to_first(h, j).wait_recv()
+                return running + first_in[j, pl.ds(0, chunk), columns[h]]
+
+            return lax.fori_loop(
+                0,
+                n_first - 1,
+                add_first,
+                part[out_rows(first), columns[h]] + arrived[rows_of(first), columns[h]],
+            )
+
+        def start_chunks(h):
+            @pl.loop(0, n_first - 1)
+            def _(j):
+                chunk_out(h, j).start()
 
         if direct:
-            whole_in[second] = near
-
-            @pl.loop(0, n_second - 1)
-            def _(j):
-                whole_to(j).start()
-
-            @pl.loop(0, n_second - 1)
-            def _(j):
-                whole_to(j).wait_recv()
-
-            total[out_rows(first), :] = lax.fori_loop(
-                1, n_second, lambda j, running: running + whole_in[j], whole_in[0]
-            )
+            for h in range(2):
+                whole_in[second, :, columns[h]] = near(h)
+
+                @pl.loop(0, n_second - 1)
+                def _(j):
+                    whole_to(h, j).start()
+
+            for h in range(2):
+
+                @pl.loop(0, n_second - 1)
+                def _(j):
+                    whole_to(h, j).wait_recv()
+
+                total[out_rows(first), columns[h]] = lax.fori_loop(
+                    1,
+                    n_second,
+                    lambda j, running: running + whole_in[j, :, columns[h]],
+                    whole_in[0, :, columns[h]],
+                )
+                start_chunks(h)
         else:
-            chunk_sum[...] = near
-
-            @pl.loop(0, n_second - 1)
-            def _(j):
-                to_second(j).start()
+            def in_half(h, j):
+                return lax.rem(second_target(j), 2) == h
+
+            for h in range(2):
+                chunk_sum[:, columns[h]] = near(h)
+
+                @pl.loop(0, n_second - 1)
+                def _(j):
+                    @pl.when(in_half(h, j))
+                    def _():
+                        to_second(j).start()
 
             def add_second(j, running):
                 to_second(j).wait_recv()
@@ -472,30 +497,36 @@
             def _(j):
                 tile_out(j).start()
 
-            @pl.loop(0, n_second - 1)
+            for h in range(2):
+
+                @pl.loop(0, n_second - 1)
+                def _(j):
+                    @pl.when(in_half(h, j))
+                    def _():
+                        tile_out(j).wait_recv()
+
+                start_chunks(h)
+
+        over(n_first - 1, first).start()
+
+        @pl.loop(0, n_first - 1)
+        def _(j):
+            chunk_out(0, j).wait_recv()
+            chunk_out(1, j).wait_recv()
+            over(j, lax.rem(first + n_first - distance(n_first, j), n_first)).start()
+
+        for h in range(2):
+
+            @pl.loop(0, n_first - 1)
             def _(j):
-                tile_out(j).wait_recv()
-
-        @pl.loop(0, n_first - 1)
-        def _(j):
-            chunk_out(j).start()
-
-        over(n_first - 1, first).start()
-
-        @pl.loop(0, n_first - 1)
-        def _(j):
-            chunk_out(j).wait_recv()
-            over(j, lax.rem(first + n_first - distance(n_first, j), n_first)).start()
-
-        @pl.loop(0, n_first - 1)
-        def _(j):
-            to_first(j).wait_send()
-            chunk_out(j).wait_send()
+                to_first(h, j).wait_send()
+                chunk_out(h, j).wait_send()
 
         @pl.loop(0, n_second - 1)
         def _(j):
             if direct:
-                whole_to(j).wait_send()
+                whole_to(0, j).wait_send()
+                whole_to(1, j).wait_send()
             else:
                 to_second(j).wait_send()
                 tile_out(j).wait_send()
@@ -572,14 +603,14 @@
             pltpu.VMEM((half_rows, rank), f32),
             pltpu.VMEM((half_rows, rank), f32),
             pltpu.VMEM((chunk_y, rank), f32),
-            pltpu.VMEM((most - 1, chunk, rank), f32),
+            pltpu.VMEM((most, chunk, rank), f32),
             pltpu.VMEM((most - 1, 8, 128), f32),
             pltpu.VMEM((along_y, chunk_z, rank), f32),
             DMA((5,)),
             DMA((20,)),
             DMA((20,)),
         ]
-        + [DMA((most,))] * 12,
+        + [DMA((2 * most,))] * 12,
         compiler_params=pltpu.CompilerParams(collective_id=0, has_side_effects=True),
     )(*tiles, linear, squares, user_factor, item_factor)
 
@@ -621,7 +652,7 @@
         user_devices // (ALONG_Z * CORES),
         ALONG_Z,
     )
-    user_grad = user_sum.reshape(user_blocks * width, rank) * width ** (-0.5)
+    user_grad = user_sum.reshape(user_blocks * width, rank)
     new_user_linear, new_user_squares = ftrl_state(
         user_grad, user_linear, user_squares, user_factor
     )

time: 81.1 us -> 79.6 us (0.982)
  Pallas kernels: 73.6 us -> 72.5 us
    mul x1 -> x0, other arithmetic: 1.47 us -> none  [on_device(): user_grad = user_sum.reshape(user_blocks * width, rank) * width ** (-0.5)]
    convert_element_type x2, other arithmetic: 4.14 us -> 5.49 us  [ftrl_factor(): return weight.astype(jnp.bfloat16)]
    pallas_call x1, Pallas kernels: 73.6 us -> 72.5 us  [both_totals(): pl.pallas_call(functools.partial(both_kernel, along_z, width ** (-0.5)),...]
where the time goes in v4:
time: 79.6 us; the launch traced here: 79.4 us
  Pallas kernels  72.5 us (91%)
  other arithmetic  5.49 us (7%)
  between operations  1.38 us (2%)
    pallas_call x1, Pallas kernels, both_totals(): pl.pallas_call(functools.partial(both_kernel, along_z, width ** (-0.5)),...  72.5 us
    convert_element_type x2, other arithmetic, ftrl_factor(): return weight.astype(jnp.bfloat16)  5.49 us

profile of v4, /device:TPU:1, one launch (start us, length us, event | category | flops | bytes accessed | tf_op | source)
XLA Modules:
  0.0 79.4 jit_solution(887431682677522741)
XLA Ops:
  1.3 0.0 copy-start
  1.3 0.0 copy-start.1
  1.3 0.0 copy-start.2
  1.3 72.5 %both_totals.1 = (f32[4,256,256]{2,1,0:T(8,128)}, f32[768,256]{1,0:T(8,128)}) custom-call(s32[8]{0:T(128)} %bitcast.25, s32[8]{0:T(128)} %bitcast.26, s32[1]{0:T(128)} %bitcast.18.tile_count, bf16[8,256,256]{2,1,0:T(8,128)(2,1)} %bitcast.23, bf16[8,256,256]{2,1,0:T(8,128)(2,1)} %bitcast.24, f32[4,256,256]{2,1,0:T(8,128)} %bitcast.20, ...), custom_call_target="tpu_custom_call" | custom-call | tf_op jit(solution)/shard_map/both_totals/pallas_call | solution.py:584
  73.9 0.0 copy-done
  73.9 0.0 copy-done.1
  73.9 0.0 copy-done.2
  73.9 0.0 copy-start.3
  73.9 0.0 copy-start.4
  73.9 0.0 copy-start.5
  73.9 0.0 copy-start.6
  73.9 3.6 %select_convert_fusion = (bf16[1024,256]{1,0:T(8,128)(2,1)}, f32[1024,256]{1,0:T(8,128)}, f32[1024,256]{1,0:T(8,128)}) fusion(bf16[1024,256]{1,0:T(8,128)(2,1)S(1)} %copy-done.2, f32[1024,256]{1,0:T(8,128)S(1)} %copy-done, f32[1024,256]{1,0:T(8,128)S(1)} %copy-done.1, f32[4,256,256]{2,1,0:T(8,128)} %get-tuple-element.8), kind=kLoop, calls=%fused_computation.4 | loop fusion | flops 5242880 | bytes 6291456 | tf_op jit(solution)/shard_map/convert_element_type | solution.py:32
  77.5 0.0 copy-done.3
  77.5 0.0 copy-done.4
  77.6 0.0 copy-done.5
  77.6 0.0 copy-done.6
  77.6 1.9 %select_convert_fusion.1 = (bf16[768,256]{1,0:T(8,128)(2,1)}, f32[768,256]{1,0:T(8,128)}, f32[768,256]{1,0:T(8,128)}) fusion(bf16[768,256]{1,0:T(8,128)(2,1)S(1)} %copy-done.3, f32[768,256]{1,0:T(8,128)S(1)} %copy-done.4, f32[768,256]{1,0:T(8,128)S(1)} %copy-done.5, f32[768,256]{1,0:T(8,128)S(1)} %copy-done.6), kind=kLoop, calls=%fused_computation.6 | loop fusion | flops 4128768 | bytes 4718592 | tf_op jit(solution)/shard_map/convert_element_type | solution.py:32
Async XLA Ops:
  1.3 72.6 %copy-start = (f32[1024,256]{1,0:T(8,128)S(1)}, f32[1024,256]{1,0:T(8,128)}, u32[]{:S(2)}) copy-start(f32[1024,256]{1,0:T(8,128)} %param.18) | copy-start | bytes 3145732
  1.3 72.6 %copy-start.1 = (f32[1024,256]{1,0:T(8,128)S(1)}, f32[1024,256]{1,0:T(8,128)}, u32[]{:S(2)}) copy-start(f32[1024,256]{1,0:T(8,128)} %param.17) | copy-start | bytes 3145732
  1.3 72.6 %copy-start.2 = (bf16[1024,256]{1,0:T(8,128)(2,1)S(1)}, bf16[1024,256]{1,0:T(8,128)(2,1)}, u32[]{:S(2)}) copy-start(bf16[1024,256]{1,0:T(8,128)(2,1)} %param.16) | copy-start | bytes 1572868
  73.9 3.7 %copy-start.3 = (bf16[768,256]{1,0:T(8,128)(2,1)S(1)}, bf16[768,256]{1,0:T(8,128)(2,1)}, u32[]{:S(2)}) copy-start(bf16[768,256]{1,0:T(8,128)(2,1)} %param.19) | copy-start | bytes 1179652
  73.9 3.6 %copy-start.4 = (f32[768,256]{1,0:T(8,128)S(1)}, f32[768,256]{1,0:T(8,128)}, u32[]{:S(2)}) copy-start(f32[768,256]{1,0:T(8,128)} %param.21) | copy-start | bytes 2359300
  73.9 3.6 %copy-start.5 = (f32[768,256]{1,0:T(8,128)S(1)}, f32[768,256]{1,0:T(8,128)}, u32[]{:S(2)}) copy-start(f32[768,256]{1,0:T(8,128)} %param.20) | copy-start | bytes 2359300
  73.9 3.6 %copy-start.6 = (f32[768,256]{1,0:T(8,128)S(1)}, f32[768,256]{1,0:T(8,128)}, u32[]{:S(2)}) copy-start(f32[768,256]{1,0:T(8,128)} %get-tuple-element.9) | copy-start | bytes 2359300
